TPU v7x, 32 devices: a whole 2x2x4 slice. The times are simulated.
32 devices in a mesh: rep: 8 (over y, x, core), tp: 4 (over z).
Axes of the slice: x: 2, y: 2, z: 4, core: 2. Of those that a mesh axis runs over, the one named last changes fastest.
Arguments:
- context: bfloat16 [16384, 5120], P('rep', 'tp'), may hold values from -6 to 6
- out_grad: bfloat16 [16384, 5120], P('rep', 'tp'), may hold values from -6 to 6
- rewards: int32 [8, 32], P(None, 'rep'), may hold values from 0 to 1
- master: float32 [5120, 5120], P('rep', 'tp'), may hold values from -0.078125 to 0.078125
- first_moment: float32 [5120, 5120], P('rep', 'tp'), may hold values from -0.046875 to 0.046875
- second_moment: float32 [5120, 5120], P('rep', 'tp'), may hold values from 6.1035155e-07 to 6.1035156e-05
- inputs: bfloat16 [4, 256, 5120], P(None, 'rep'), may hold values from -6 to 6
- w_query: bfloat16 [5120, 5120], P(None, 'tp'), may hold values from -0.078125 to 0.078125
- w_key: bfloat16 [5120, 1024], P(None, 'tp'), may hold values from -0.078125 to 0.078125
- w_value: bfloat16 [5120, 1024], P(None, 'tp'), may hold values from -0.078125 to 0.078125
- cache_keys: bfloat16 [256, 256, 1024], P('rep', None, 'tp'), may hold values from -400 to 400
- cache_values: bfloat16 [256, 256, 1024], P('rep', None, 'tp'), may hold values from -24 to 24
- lengths: int32 [32], P('rep'), may hold values from 64 to 256
Outputs:
- decoded: bfloat16 [4, 256, 5120], P(None, 'rep')
- adam_step: float32 [5120, 5120], P('rep', 'tp')
All inputs are finite; a program needn't handle non-finite values.
Results may differ from a plain program's by a relative error of at most 0.0088.
Values may be sent and summed in bfloat16 or wider, within the bound.
No kernel may reach another device: no remote copies, remote signals or barrier semaphores. Data moves between devices by JAX's collectives and lax.ppermute only.
A program may use at most 192 MiB of HBM per device.

v0:
```python
import jax
import jax.numpy as jnp
from jax import lax
from jax.sharding import PartitionSpec as P

HEAD_DIM = 128
rope_base = 1000000.0
first_beta = 0.9
second_beta = 0.95
adam_epsilon = 1e-08
step_count = 10
learn_rate = 0.001


def rotate(vectors, positions):
    half_dim = vectors.shape[-1] // 2
    frequency = rope_base ** (-2.0 * jnp.arange(half_dim, dtype=jnp.float32) / vectors.shape[-1])
    angles = positions[..., None].astype(jnp.float32) * frequency
    cosine_table = jnp.cos(angles)
    sine_table = jnp.sin(angles)
    former = vectors[..., :half_dim]
    latter = vectors[..., half_dim:]
    return jnp.concatenate(
        [former * cosine_table - latter * sine_table, latter * cosine_table + former * sine_table],
        axis=-1,
    )


def attend(queries, old_keys, old_values, new_keys, new_values, live_mask):
    score_scale = HEAD_DIM ** (-0.5)
    step_total = queries.shape[0]
    cache_scores = (
        jnp.einsum("tsgqd,scgd->tsgqc", queries, old_keys, preferred_element_type=jnp.float32)
        * score_scale
    )
    cache_scores = jnp.where(live_mask[None, :, None, None, :], cache_scores, -1e30)
    recent = (
        jnp.einsum("tsgqd,usgd->tsgqu", queries, new_keys, preferred_element_type=jnp.float32)
        * score_scale
    )
    causal = jnp.arange(step_total)[:, None] >= jnp.arange(step_total)[None, :]
    recent = jnp.where(causal[:, None, None, None, :], recent, -1e30)
    row_peak = jnp.maximum(jnp.max(cache_scores, axis=-1), jnp.max(recent, axis=-1))[..., None]
    cache_exp = jnp.exp(cache_scores - row_peak)
    recent_exp = jnp.exp(recent - row_peak)
    denominator = jnp.sum(cache_exp, axis=-1, keepdims=True) + jnp.sum(
        recent_exp, axis=-1, keepdims=True
    )
    cache_weight = (cache_exp / denominator).astype(jnp.bfloat16)
    recent_weight = (recent_exp / denominator).astype(jnp.bfloat16)
    attended = jnp.einsum(
        "tsgqc,scgd->tsgqd", cache_weight, old_values, preferred_element_type=jnp.float32
    )
    attended = attended + jnp.einsum(
        "tsgqu,usgd->tsgqd", recent_weight, new_values, preferred_element_type=jnp.float32
    )
    return attended.astype(jnp.bfloat16)


def per_device(
    context,
    out_grad,
    rewards,
    master,
    first_moment,
    second_moment,
    inputs,
    w_query,
    w_key,
    w_value,
    cache_keys,
    cache_values,
    lengths,
):
    replicas = lax.axis_size("rep")
    prompt_count, local_group = rewards.shape
    totals = lax.psum(jnp.sum(rewards, axis=1), "rep")
    group_size = local_group * replicas
    advantage = rewards.astype(jnp.float32) - totals.astype(jnp.float32)[:, None] / group_size
    token_local = context.shape[0]
    per_token = jnp.repeat(advantage.reshape(-1), token_local // (prompt_count * local_group)) / (
        token_local * replicas
    )
    scaled = (out_grad.astype(jnp.float32) * per_token[:, None]).astype(jnp.bfloat16)
    features = lax.all_gather(context, "tp", axis=1, tiled=True)
    gradient = lax.psum_scatter(
        lax.dot_general(
            features, scaled, (((0,), (0,)), ((), ())), preferred_element_type=jnp.float32
        ).astype(jnp.bfloat16),
        "rep",
        scatter_dimension=0,
        tiled=True,
    ).astype(jnp.float32)
    moment_new = first_beta * first_moment + (1.0 - first_beta) * gradient
    square_new = second_beta * second_moment + (1.0 - second_beta) * gradient * gradient
    adam_step = (
        moment_new
        / (1.0 - first_beta**step_count)
        / (jnp.sqrt(square_new / (1.0 - second_beta**step_count)) + adam_epsilon)
    )
    weight = (master - learn_rate * adam_step).astype(jnp.bfloat16)
    step_total, seq_local, model_width = inputs.shape
    local_heads = w_query.shape[1] // HEAD_DIM
    local_kv = w_key.shape[1] // HEAD_DIM
    flat_rows = inputs.reshape(step_total * seq_local, model_width)
    queries = jnp.dot(flat_rows, w_query, preferred_element_type=jnp.float32).reshape(
        step_total, seq_local, local_heads, HEAD_DIM
    )
    key_new = jnp.dot(flat_rows, w_key, preferred_element_type=jnp.float32).reshape(
        step_total, seq_local, local_kv, HEAD_DIM
    )
    value_new = (
        jnp.dot(flat_rows, w_value, preferred_element_type=jnp.float32)
        .reshape(step_total, seq_local, local_kv, HEAD_DIM)
        .astype(jnp.bfloat16)
    )
    seq_length = jnp.repeat(lengths, seq_local // lengths.shape[0])
    positions = seq_length[None, :] + jnp.arange(step_total, dtype=jnp.int32)[:, None]
    queries = rotate(queries, positions[:, :, None]).astype(jnp.bfloat16)
    queries = queries.reshape(step_total, seq_local, local_kv, local_heads // local_kv, HEAD_DIM)
    key_new = rotate(key_new, positions[:, :, None]).astype(jnp.bfloat16)
    slot_total = cache_keys.shape[1]
    old_keys = cache_keys.reshape(seq_local, slot_total, local_kv, HEAD_DIM)
    old_values = cache_values.reshape(seq_local, slot_total, local_kv, HEAD_DIM)
    live_mask = jnp.arange(slot_total, dtype=jnp.int32)[None, :] < seq_length[:, None]
    attended = attend(queries, old_keys, old_values, key_new, value_new, live_mask)
    attended = attended.reshape(step_total * seq_local, local_heads * HEAD_DIM)
    all_heads = lax.all_gather(attended, "tp", axis=1, tiled=True)
    feature_rows = lax.all_to_all(all_heads, "rep", split_axis=1, concat_axis=0, tiled=True)
    own_columns = lax.psum_scatter(
        jnp.dot(feature_rows, weight, preferred_element_type=jnp.float32),
        "rep",
        scatter_dimension=0,
        tiled=True,
    )
    decoded = lax.all_gather(own_columns.astype(jnp.bfloat16), "tp", axis=1, tiled=True)
    return (decoded.reshape(step_total, seq_local, model_width), adam_step)


def solution(mesh):
    placed = (
        P("rep", "tp"),
        P("rep", "tp"),
        P(None, "rep"),
        P("rep", "tp"),
        P("rep", "tp"),
        P("rep", "tp"),
        P(None, "rep", None),
        P(None, "tp"),
        P(None, "tp"),
        P(None, "tp"),
        P("rep", None, "tp"),
        P("rep", None, "tp"),
        P("rep"),
    )
    return jax.shard_map(
        per_device,
        mesh=mesh,
        in_specs=placed,
        out_specs=(P(None, "rep", None), P("rep", "tp")),
        check_vma=False,
    )
```

profile of v0, /device:TPU:0, one launch (start us, length us, event | category | flops | bytes accessed | tf_op | source)
XLA Modules:
  0.0 632.1 jit_solution(17506920975322697041)
XLA Ops:
  8.1 4.4 copy.64
  12.5 4.5 copy.69
  17.0 7.3 %reshape.131 = bf16[32,256,2,128]{3,2,1,0:T(2,128)(2,1)} reshape(bf16[32,256,256]{2,1,0:T(8,128)(2,1)} %param.23) | data formatting | bytes 8388608 | tf_op jit(solution)/shard_map/reshape | solution.py:123
  24.3 7.2 %reshape.132 = bf16[32,256,2,128]{3,2,1,0:T(2,128)(2,1)} reshape(bf16[32,256,256]{2,1,0:T(8,128)(2,1)} %param.24) | data formatting | bytes 8388608 | tf_op jit(solution)/shard_map/reshape | solution.py:124
  31.5 17.8 %copy.41 = bf16[5120,1280]{0,1:T(8,128)(2,1)} copy(bf16[5120,1280]{1,0:T(8,128)(2,1)} %param.20) | data formatting | bytes 26214400 | tf_op args[7]
  49.6 7.2 %fusion.27 = f32[4,32,10,128]{3,1,2,0:T(8,128)S(1)} fusion(bf16[10,128,5120,1]{2,1,0,3:T(8,128)(2,1)} %bitcast.73, bf16[4,32,5120]{2,1,0:T(8,128)(2,1)S(1)} %copy-done), kind=kOutput, calls=%fused_computation.34 | convolution fusion | flops 1677721600 | bytes 15073280 | tf_op jit(solution)/shard_map/dot_general | solution.py:106
  59.9 2.6 fusion.55
  70.9 9.6 %psum.7 = s32[8]{0:T(128)S(1)} all-reduce(s32[8]{0:T(128)S(1)} %reduce_sum.29), channel_id=1, replica_groups=mesh['rep'=8,'tp'=4] {'rep'}, use_global_device_ids=true, to_apply=%region_5.6 | all-reduce | flops 8 | bytes 64 | tf_op jit(solution)/shard_map/psum | solution.py:77
  80.9 288.3 %all-gather.6.cloned.1.call-done = bf16[2048,5120]{1,0:T(8,128)(2,1)} async-done(((bf16[2048,1280]{1,0:T(8,128)(2,1)}), bf16[2048,5120]{1,0:T(8,128)(2,1)}) %all-gather.6.cloned.1.call-update) | async-done | bytes 20971536 | tf_op jit(solution)/shard_map/all_gather | solution.py:85
  369.1 34.5 %fusion = bf16[5120,1280]{0,1:T(8,128)(2,1)} fusion(bf16[2048,5120]{1,0:T(8,128)(2,1)} %all-gather.6.cloned.1.call-done, bf16[2048,1280]{1,0:T(8,128)(2,1)} %param.14, f32[2048]{0:T(1024)S(1)} %div.60), kind=kOutput, calls=%fused_computation.1 | convolution fusion | flops 26857963520 | bytes 39329792 | tf_op jit(solution)/shard_map/dot_general | solution.py:87
  403.7 17.6 %copy.72 = bf16[5120,1280]{1,0:T(8,128)(2,1)} copy(bf16[5120,1280]{0,1:T(8,128)(2,1)} %fusion) | data formatting | bytes 26214400
  421.4 2.5 copy.94
  423.9 3.7 all-to-all-start
  427.6 4.9 copy.55
  432.5 5.1 copy.52
  437.5 4.8 copy.54
  442.3 72.5 %reduce-scatter.7.cloned.1.call-done = bf16[640,1280]{1,0:T(8,128)(2,1)} async-done(((bf16[5120,1280]{1,0:T(8,128)(2,1)}), bf16[640,1280]{1,0:T(8,128)(2,1)}) %reduce-scatter.7.cloned.1.call-update) | async-done | bytes 1638416
  514.8 2.8 copy.73
  517.6 6.7 %fusion.8 = f32[640,1280]{0,1:T(8,128)} fusion(bf16[640,1280]{0,1:T(8,128)(2,1)S(1)} %copy.73, f32[640,1280]{0,1:T(8,128)} %copy.54, f32[640,1280]{0,1:T(8,128)} %copy.52), kind=kLoop, calls=%fused_computation.12 | loop fusion | flops 9830400 | bytes 11468800 | tf_op jit(solution)/shard_map/div | solution.py:97
  524.4 7.5 %fusion.14 = f32[1024,1280]{1,0:T(8,128)} fusion(bf16[1024,640]{1,0:T(8,128)(2,1)S(1)} %bitcast.74, f32[640,1280]{0,1:T(8,128)} %copy.55, f32[640,1280]{0,1:T(8,128)} %fusion.8), kind=kOutput, calls=%fused_computation.23 | convolution fusion | flops 1680179200 | bytes 13107200 | tf_op jit(solution)/shard_map/dot_general | solution.py:131
  531.9 56.6 %reduce-scatter.5.cloned.1.call-done = f32[128,1280]{1,0:T(8,128)} async-done(((f32[1024,1280]{1,0:T(8,128)}), f32[128,1280]{1,0:T(8,128)}) %reduce-scatter.5.cloned.1.call-update) | async-done | bytes 655376 | tf_op jit(solution)/shard_map/reduce_scatter | solution.py:130
  590.4 4.7 copy.56
  595.1 28.0 %all-gather.8.cloned.1.call-done = bf16[128,5120]{1,0:T(8,128)(2,1)} async-done(((bf16[128,1280]{1,0:T(8,128)(2,1)}), bf16[128,5120]{1,0:T(8,128)(2,1)}) %all-gather.8.cloned.1.call-update) | async-done | bytes 1310736 | tf_op jit(solution)/shard_map/all_gather | solution.py:136
  623.1 2.5 copy.96
  (59 shorter events, 15.0 us)
Async XLA Ops:
  7.2 42.5 %copy-start = (bf16[4,32,5120]{2,1,0:T(8,128)(2,1)S(1)}, bf16[4,32,5120]{2,1,0:T(8,128)(2,1)}, u32[]{:S(2)}) copy-start(bf16[4,32,5120]{2,1,0:T(8,128)(2,1)} %param.19) | copy-start | bytes 3932164
  7.2 0.8 copy-start.7
  7.2 362.0 %all-gather.6.cloned.1.call-start = ((), (), s32[]{:S(2)}) async-start(), calls=%async_computation.4 | async-start | bytes 26214400 | tf_op jit(solution)/shard_map/all_gather | solution.py:85
  7.9 413.4 %all-gather.4.cloned.1.call-start = ((), (), s32[]{:S(2)}) async-start(), calls=%async_computation.3 | async-start | bytes 1638400 | tf_op jit(solution)/shard_map/all_gather | solution.py:128
  56.8 1.7 copy-start.5
  58.6 3.9 copy-start.2
  64.0 1.9 copy-start.4
  65.9 2.2 copy-start.3
  68.2 2.7 copy-start.6
  70.9 443.9 %reduce-scatter.7.cloned.1.call-start = ((), (), s32[]{:S(2)}) async-start(), calls=%async_computation.7 | async-start | bytes 14745600
  423.9 100.5 %all-to-all-start = ((bf16[128,8,640]{2,0,1:T(8,128)(2,1)}), bf16[128,8,640]{2,0,1:T(8,128)(2,1)S(1)}, u32[]{:S(2)}, u32[]{:S(2)}) async-start(bf16[128,8,640]{2,0,1:T(8,128)(2,1)} %bitcast.71), calls=%async_computation | async-start | bytes 2621440 | tf_op jit(solution)/shard_map/all_to_all | solution.py:129
  427.5 161.0 %reduce-scatter.5.cloned.1.call-start = ((), (), s32[]{:S(2)}) async-start(), calls=%async_computation.5 | async-start | bytes 5898240 | tf_op jit(solution)/shard_map/reduce_scatter | solution.py:130
  531.9 91.2 %all-gather.8.cloned.1.call-start = ((), (), s32[]{:S(2)}) async-start(), calls=%async_computation.6 | async-start | bytes 1638400 | tf_op jit(solution)/shard_map/all_gather | solution.py:136
  590.4 35.1 %copy-start.1 = (bf16[4,32,5120]{2,1,0:T(8,128)(2,1)S(1)}, bf16[4,32,5120]{2,1,0:T(8,128)(2,1)}, u32[]{:S(2)}) copy-start(bf16[4,32,5120]{2,1,0:T(8,128)(2,1)} %param.19) | copy-start | bytes 3932164
Sparse Core Ops, SparseCore 0:
  9.6 359.5 all-gather.5
  371.3 31.0 all-gather.3
  421.5 93.2 reduce-scatter.6
  532.0 56.5 reduce-scatter.4
  590.5 32.5 all-gather.7
where the time goes:
time: 634 us; the launch traced here: 632 us
  waiting for transfers between devices  446 us (70%)
  local copies, waits for them, and re-layouts  89.8 us (14%)
  matrix products  57.3 us (9%)
  between operations  14 us (2%)
  other arithmetic  11.4 us (2%)
  blocking collectives  9.6 us (2%)
    all_gather x1, waiting for transfers between devices, per_device(): features = lax.all_gather(context, 'tp', axis=1, tiled=True)  288 us
    unnamed x6, waiting for transfers between devices  73.3 us
    unnamed x24, local copies, waits for them, and re-layouts  61.9 us
    reduce_scatter x1, waiting for transfers between devices, per_device(): lax.psum_scatter(jnp.dot(feature_rows, weight, preferred_element_type=jnp...  56.6 us
    dot_general x1, matrix products, per_device(): lax.dot_general(features, scaled, (((0,), (0,)), ((), ())), preferred_ele...  34.5 us
    all_gather x1, waiting for transfers between devices, per_device(): lax.all_gather(own_columns.astype(jnp.bfloat16), 'tp', axis=1, tiled=True)  28 us
  transfers between devices with their start and end apart: 6, of which 4 were waited for; matrix products, arithmetic and copies ran while one was open for 23% of the time, Pallas kernels for 0%

commit v1 on v0

--- a/solution.py
+++ b/solution.py
@@ -82,7 +82,7 @@
         token_local * replicas
     )
     scaled = (out_grad.astype(jnp.float32) * per_token[:, None]).astype(jnp.bfloat16)
-    features = lax.all_gather(context, "tp", axis=1, tiled=True)
+    features = jnp.concatenate(lax.all_gather(context, "tp"), axis=1)
     gradient = lax.psum_scatter(
         lax.dot_general(
             features, scaled, (((0,), (0,)), ((), ())), preferred_element_type=jnp.float32

time: 634 us -> 663 us (1.046)
  local copies, waits for them, and re-layouts: 89.8 us -> 117 us
    reshape x0 -> x1, local copies, waits for them, and re-layouts: none -> 27.2 us  [per_device(): features = jnp.concatenate(lax.all_gather(context, 'tp'), axis=1)]
  transfers between devices with their start and end apart: 6 -> 6, of which waited for: 4 -> 4; matrix products, arithmetic and copies ran while one was open for 23% -> 26% of each run, Pallas kernels for 0% -> 0%
where the time goes in v1:
time: 663 us; the launch traced here: 661 us
  waiting for transfers between devices  446 us (67%)
  local copies, waits for them, and re-layouts  117 us (18%)
  matrix products  58.5 us (9%)
  between operations  14 us (2%)
  other arithmetic  11.4 us (2%)
  blocking collectives  9.62 us (1%)
    all_gather x1, waiting for transfers between devices, per_device(): features = jnp.concatenate(lax.all_gather(context, 'tp'), axis=1)  288 us
    unnamed x6, waiting for transfers between devices  72.7 us
    unnamed x24, local copies, waits for them, and re-layouts  62.2 us
    reduce_scatter x1, waiting for transfers between devices, per_device(): lax.psum_scatter(jnp.dot(feature_rows, weight, preferred_element_type=jnp...  56.6 us
    dot_general x1, matrix products, per_device(): lax.dot_general(features, scaled, (((0,), (0,)), ((), ())), preferred_ele...  35.7 us
    all_gather x1, waiting for transfers between devices, per_device(): lax.all_gather(own_columns.astype(jnp.bfloat16), 'tp', axis=1, tiled=True)  28 us
    reshape x1, local copies, waits for them, and re-layouts, per_device(): features = jnp.concatenate(lax.all_gather(context, 'tp'), axis=1)  27.2 us
  transfers between devices with their start and end apart: 6, of which 4 were waited for; matrix products, arithmetic and copies ran while one was open for 26% of the time, Pallas kernels for 0%

profile of v1, /device:TPU:0, one launch (start us, length us, event | category | flops | bytes accessed | tf_op | source)
XLA Modules:
  0.0 660.5 jit_solution(18140882096426742484)
XLA Ops:
  8.1 4.4 copy.82
  12.5 4.5 copy.87
  17.0 7.3 %reshape.137 = bf16[32,256,2,128]{3,2,1,0:T(2,128)(2,1)} reshape(bf16[32,256,256]{2,1,0:T(8,128)(2,1)} %param.23) | data formatting | bytes 8388608 | tf_op jit(solution)/shard_map/reshape | solution.py:123
  24.3 7.2 %reshape.138 = bf16[32,256,2,128]{3,2,1,0:T(2,128)(2,1)} reshape(bf16[32,256,256]{2,1,0:T(8,128)(2,1)} %param.24) | data formatting | bytes 8388608 | tf_op jit(solution)/shard_map/reshape | solution.py:124
  31.5 17.8 %copy.58 = bf16[5120,1280]{0,1:T(8,128)(2,1)} copy(bf16[5120,1280]{1,0:T(8,128)(2,1)} %param.20) | data formatting | bytes 26214400 | tf_op args[7]
  49.6 7.2 %fusion.27 = f32[4,32,10,128]{3,1,2,0:T(8,128)S(1)} fusion(bf16[10,128,5120,1]{2,1,0,3:T(8,128)(2,1)} %bitcast.79, bf16[4,32,5120]{2,1,0:T(8,128)(2,1)S(1)} %copy-done), kind=kOutput, calls=%fused_computation.34 | convolution fusion | flops 1677721600 | bytes 15073280 | tf_op jit(solution)/shard_map/dot_general | solution.py:106
  59.9 2.6 fusion.55
  70.9 9.6 %psum.7 = s32[8]{0:T(128)S(1)} all-reduce(s32[8]{0:T(128)S(1)} %reduce_sum.29), channel_id=1, replica_groups=mesh['rep'=8,'tp'=4] {'rep'}, use_global_device_ids=true, to_apply=%region_5.6 | all-reduce | flops 8 | bytes 64 | tf_op jit(solution)/shard_map/psum | solution.py:77
  80.9 288.3 %all-gather.9.cloned.1.call-done = bf16[8192,1280]{1,0:T(8,128)(2,1)} async-done(((bf16[2048,1280]{1,0:T(8,128)(2,1)}), bf16[8192,1280]{1,0:T(8,128)(2,1)}) %all-gather.9.cloned.1.call-update) | async-done | bytes 20971536 | tf_op jit(solution)/shard_map/all_gather | solution.py:85
  369.2 27.2 %copy.71 = bf16[2048,4,1280]{0,2,1:T(8,128)(2,1)} copy(bf16[2048,4,1280]{2,0,1:T(8,128)(2,1)} %bitcast.76) | data formatting | bytes 41943040 | tf_op jit(solution)/shard_map/reshape | solution.py:85
  396.4 35.7 %fusion = bf16[5120,1280]{0,1:T(8,128)(2,1)} fusion(bf16[2048,5120]{0,1:T(8,128)(2,1)} %bitcast.77, bf16[2048,1280]{1,0:T(8,128)(2,1)} %param.14, f32[2048]{0:T(1024)S(1)} %div.60), kind=kOutput, calls=%fused_computation.1 | convolution fusion | flops 26857963520 | bytes 39329792 | tf_op jit(solution)/shard_map/dot_general | solution.py:87
  432.1 17.6 %copy.90 = bf16[5120,1280]{1,0:T(8,128)(2,1)} copy(bf16[5120,1280]{0,1:T(8,128)(2,1)} %fusion) | data formatting | bytes 26214400
  449.8 2.5 copy.112
  452.3 3.7 all-to-all-start
  456.3 5.1 copy.73
  461.3 5.2 copy.69
  466.5 4.7 copy.72
  471.2 72.0 %reduce-scatter.7.cloned.1.call-done = bf16[640,1280]{1,0:T(8,128)(2,1)} async-done(((bf16[5120,1280]{1,0:T(8,128)(2,1)}), bf16[640,1280]{1,0:T(8,128)(2,1)}) %reduce-scatter.7.cloned.1.call-update) | async-done | bytes 1638416
  543.2 2.8 copy.91
  546.0 6.7 %fusion.8 = f32[640,1280]{0,1:T(8,128)} fusion(bf16[640,1280]{0,1:T(8,128)(2,1)S(1)} %copy.91, f32[640,1280]{0,1:T(8,128)} %copy.72, f32[640,1280]{0,1:T(8,128)} %copy.69), kind=kLoop, calls=%fused_computation.12 | loop fusion | flops 9830400 | bytes 11468800 | tf_op jit(solution)/shard_map/div | solution.py:97
  552.8 7.5 %fusion.14 = f32[1024,1280]{1,0:T(8,128)} fusion(bf16[1024,640]{1,0:T(8,128)(2,1)S(1)} %bitcast.80, f32[640,1280]{0,1:T(8,128)} %copy.73, f32[640,1280]{0,1:T(8,128)} %fusion.8), kind=kOutput, calls=%fused_computation.23 | convolution fusion | flops 1680179200 | bytes 13107200 | tf_op jit(solution)/shard_map/dot_general | solution.py:131
  560.3 56.6 %reduce-scatter.5.cloned.1.call-done = f32[128,1280]{1,0:T(8,128)} async-done(((f32[1024,1280]{1,0:T(8,128)}), f32[128,1280]{1,0:T(8,128)}) %reduce-scatter.5.cloned.1.call-update) | async-done | bytes 655376 | tf_op jit(solution)/shard_map/reduce_scatter | solution.py:130
  618.9 4.7 copy.74
  623.5 28.0 %all-gather.7.cloned.1.call-done = bf16[128,5120]{1,0:T(8,128)(2,1)} async-done(((bf16[128,1280]{1,0:T(8,128)(2,1)}), bf16[128,5120]{1,0:T(8,128)(2,1)}) %all-gather.7.cloned.1.call-update) | async-done | bytes 1310736 | tf_op jit(solution)/shard_map/all_gather | solution.py:136
  (60 shorter events, 17.6 us)
Async XLA Ops:
  7.2 42.5 %copy-start = (bf16[4,32,5120]{2,1,0:T(8,128)(2,1)S(1)}, bf16[4,32,5120]{2,1,0:T(8,128)(2,1)}, u32[]{:S(2)}) copy-start(bf16[4,32,5120]{2,1,0:T(8,128)(2,1)} %param.19) | copy-start | bytes 3932164
  7.2 0.8 copy-start.7
  7.2 362.0 %all-gather.9.cloned.1.call-start = ((), (), s32[]{:S(2)}) async-start(), calls=%async_computation.6 | async-start | bytes 26214400 | tf_op jit(solution)/shard_map/all_gather | solution.py:85
  7.9 441.9 %all-gather.5.cloned.1.call-start = ((), (), s32[]{:S(2)}) async-start(), calls=%async_computation.3 | async-start | bytes 1638400 | tf_op jit(solution)/shard_map/all_gather | solution.py:128
  56.8 1.7 copy-start.5
  58.6 3.9 copy-start.2
  64.0 1.9 copy-start.4
  65.9 2.2 copy-start.3
  68.2 2.7 copy-start.6
  70.9 472.3 %reduce-scatter.7.cloned.1.call-start = ((), (), s32[]{:S(2)}) async-start(), calls=%async_computation.7 | async-start | bytes 14745600
  452.3 100.5 %all-to-all-start = ((bf16[128,8,640]{2,0,1:T(8,128)(2,1)}), bf16[128,8,640]{2,0,1:T(8,128)(2,1)S(1)}, u32[]{:S(2)}, u32[]{:S(2)}) async-start(bf16[128,8,640]{2,0,1:T(8,128)(2,1)} %bitcast.75), calls=%async_computation | async-start | bytes 2621440 | tf_op jit(solution)/shard_map/all_to_all | solution.py:129
  456.0 161.0 %reduce-scatter.5.cloned.1.call-start = ((), (), s32[]{:S(2)}) async-start(), calls=%async_computation.4 | async-start | bytes 5898240 | tf_op jit(solution)/shard_map/reduce_scatter | solution.py:130
  560.3 91.2 %all-gather.7.cloned.1.call-start = ((), (), s32[]{:S(2)}) async-start(), calls=%async_computation.5 | async-start | bytes 1638400 | tf_op jit(solution)/shard_map/all_gather | solution.py:136
  618.9 35.1 %copy-start.1 = (bf16[4,32,5120]{2,1,0:T(8,128)(2,1)S(1)}, bf16[4,32,5120]{2,1,0:T(8,128)(2,1)}, u32[]{:S(2)}) copy-start(bf16[4,32,5120]{2,1,0:T(8,128)(2,1)} %param.19) | copy-start | bytes 3932164
Sparse Core Ops, SparseCore 0:
  9.6 359.5 all-gather.8
  371.3 31.0 all-gather.4
  449.9 93.2 reduce-scatter.6
  560.4 56.5 reduce-scatter.4
  619.0 32.5 all-gather.6
